TPU v7x, 256 devices: a whole 4x4x8 slice. The times are simulated.
256 devices in a mesh: elem: 64 (over y, z, core), snap: 4 (over x).
Axes of the slice: x: 4, y: 4, z: 8, core: 2. Of those that a mesh axis runs over, the one named last changes fastest.
Arguments:
- node_basis: bfloat16 [65536, 1536], P('elem'), may hold values from -0.25 to 0.25
- stiff_terms: bfloat16 [16, 24, 24], replicated, may hold values from -1.25 to 1.25
- reduced_coords: bfloat16 [512, 32], P(None, 'snap'), may hold values from -6 to 6
- sample_list: int32 [512], replicated, may hold values from 0 to 2047, as said below
- connectivity: int32 [2048, 8], replicated, may hold values from -1 to 65535, as said below
- node_slot: int32 [65536], replicated, may hold values from 0 to 65535, as said below
- elem_device: int32 [512], replicated, may hold values from 0 to 63, as said below
Outputs:
- ortho_panel: float32 [1024, 512, 512], P('elem', 'snap')
- triangle_factor: float32 [512, 512], P('elem')
Inputs may be any that keep to these rules, and one draw needn't show every extreme that they name: `sample_list`: distinct element ids. `connectivity`: each element lists 4, 6 or 8 live nodes first and -1 after them; the live nodes of one element are owned by distinct indices of elem (owner = node_slot // 1024); for every index d of elem and every owner o, at most 2 sampled elements computed on d have a live node owned by o, and some pair (d, o) reaches 2. `node_slot`: a permutation. `elem_device`: each index of elem computes at most 16 sampled elements; some index computes exactly 16.
All inputs are finite; a program needn't handle non-finite values.
Results may differ from a plain program's by a relative error of at most 0.0056.
Values may be sent and summed in bfloat16 or wider, within the bound.
A program may use at most 64 MiB of HBM per device.

v0:
```python
import jax
import jax.numpy as jnp
from jax import lax
from jax.sharding import PartitionSpec as P

MODES = 512
ENODES = 8
NDOF = 3


def shards(
    node_basis, stiff_terms, reduced_coords, sample_list, connectivity, node_slot, elem_device
):
    devices = lax.axis_size("elem")
    elem_rank = lax.axis_index("elem")
    node_rows = node_basis.shape[0]
    sampled = sample_list.shape[0]
    capacity = 2 * sampled // devices
    pair_bound = (capacity * ENODES + devices - 1) // devices
    node_ids = connectivity[sample_list]
    live_nodes = node_ids >= 0
    stored_rows = jnp.where(live_nodes, node_slot[jnp.maximum(node_ids, 0)], 0)
    owners = stored_rows // node_rows
    local_rows = stored_rows % node_rows
    position_ids = jnp.arange(sampled, dtype=jnp.int32)
    earlier = position_ids[None, :] < position_ids[:, None]
    same_device = elem_device[None, :] == elem_device[:, None]
    in_group = earlier & same_device
    slot_ids = jnp.sum(in_group.astype(jnp.int32), axis=1)
    owner_ids = jnp.arange(devices, dtype=jnp.int32)
    owned_mask = jnp.any(live_nodes[:, :, None] & (owners[:, :, None] == owner_ids), axis=1).astype(
        jnp.float32
    )
    ranks_by_owner = jnp.dot(
        in_group.astype(jnp.float32), owned_mask, precision=lax.Precision.HIGHEST
    ).astype(jnp.int32)
    peer_ranks = jnp.take_along_axis(ranks_by_owner, owners, axis=1)
    sending = live_nodes & (owners == elem_rank)
    target = jnp.where(sending, elem_device[:, None], devices)
    row_table = (
        jnp.full((devices, pair_bound), -1, jnp.int32)
        .at[target, peer_ranks]
        .set(local_rows, mode="drop")
    )
    send_rows = node_basis[jnp.maximum(row_table, 0)]
    outgoing = jnp.where((row_table >= 0)[:, :, None], send_rows, jnp.zeros((), jnp.bfloat16))
    incoming = lax.all_to_all(outgoing, "elem", split_axis=0, concat_axis=0, tiled=True)
    at_device = elem_device == elem_rank
    slot_index = jnp.where(at_device, slot_ids, capacity)
    slot_elem = (
        jnp.full((capacity,), sampled, jnp.int32).at[slot_index].set(position_ids, mode="drop")
    )
    slot_live = slot_elem < sampled
    picked = jnp.minimum(slot_elem, sampled - 1)
    slot_rows = incoming[owners[picked], jnp.minimum(peer_ranks[picked], pair_bound - 1)]
    slot_mask = live_nodes[picked] & slot_live[:, None]
    local_basis = jnp.where(slot_mask[:, :, None], slot_rows, jnp.zeros((), jnp.bfloat16))
    element_basis = local_basis.reshape(capacity, ENODES * NDOF, MODES)
    displaced = jnp.einsum(
        "ekm,ms->eks", element_basis, reduced_coords, preferred_element_type=jnp.float32
    ).astype(jnp.bfloat16)
    forces = jnp.einsum(
        "tkl,els->ekst", stiff_terms, displaced, preferred_element_type=jnp.float32
    ).astype(jnp.bfloat16)
    forces = forces.reshape(capacity, ENODES * NDOF, -1)
    projected = jnp.einsum(
        "ekm,ekc->emc", element_basis, forces, preferred_element_type=jnp.float32
    ).astype(jnp.bfloat16)
    banded = lax.all_to_all(projected, "snap", split_axis=1, concat_axis=2, tiled=True)
    band_rows = banded.reshape(-1, banded.shape[2])
    columns = band_rows.shape[1]
    total_rows = sampled * MODES
    partial_gram = lax.dot_general(
        band_rows, band_rows, (((0,), (0,)), ((), ())), preferred_element_type=jnp.float32
    )
    gram_matrix = lax.psum(partial_gram, ("elem", "snap"))
    gram_matrix = gram_matrix / total_rows
    lower_factor = jnp.linalg.cholesky(gram_matrix)
    identity_matrix = jnp.eye(columns, dtype=jnp.float32)
    lower_inverse = jax.scipy.linalg.solve_triangular(lower_factor, identity_matrix, lower=True)
    ortho_rows = lax.dot_general(
        band_rows.astype(jnp.float32),
        lower_inverse,
        (((1,), (1,)), ((), ())),
        precision=lax.Precision.HIGHEST,
        preferred_element_type=jnp.float32,
    )
    share = columns // devices
    upper_rows = lax.dynamic_slice_in_dim(lower_factor.T, elem_rank * share, share, 0)
    return (ortho_rows.reshape(banded.shape), upper_rows)


def solution(mesh):
    placed = (P("elem", None), P(), P(None, "snap"), P(), P(), P(), P())
    return jax.shard_map(
        shards,
        mesh=mesh,
        in_specs=placed,
        out_specs=(P("elem", "snap", None), P("elem", None)),
        check_vma=False,
    )
```

profile of v0, /device:TPU:2, one launch (start us, length us, event | category | flops | bytes accessed | tf_op | source)
XLA Modules:
  0.0 630.0 jit_solution(7660797386319666554)
XLA Ops:
  8.0 2.3 copy.109
  10.3 2.9 gather_fusion
  13.2 1.7 broadcast_maximum_fusion
  14.8 1.1 reshape.327
  15.9 23.0 %gather_fusion.2 = s32[4096]{0:T(1024)S(1)} fusion(s32[65536]{0:T(1024)S(1)} %copy-done.1, s32[4096]{0:T(1024)S(1)} %broadcast_clamp_fusion), kind=kCustom, calls=%fused_computation.2 | custom fusion | bytes 49152 | tf_op jit(solution)/shard_map/gather | solution.py:22
  40.0 1.9 add_select_fusion
  41.9 1.1 add_select_fusion.1
  43.2 1.1 reshape.379
  44.4 1.9 shift-left_or_fusion
  46.3 1.1 reshape.363
  48.0 33.0 %gather_fusion.7 = s32[4096]{0:T(1024)S(1)} fusion(s32[512,64]{0,1:T(8,128)S(1)} %convolution_convert_fusion.2, s32[4096]{0:T(1024)S(1)} %reshape.363), kind=kCustom, calls=%fused_computation.7 | custom fusion | bytes 65536 | tf_op jit(solution)/shard_map/jit(take_along_axis)/gather | solution.py:37
  81.9 2.1 compare_select_fusion.3
  88.4 15.5 %scatter_custom_fusion.1 = s32[128]{0:T(128)S(1)} fusion(s32[4096]{0:T(1024)S(1)} %reshape.377, s32[4096]{0:T(1024)S(1)} %reshape.379, s32[]{:T(128)} %constant.211.clone.1), kind=kCustom, calls=%fused_computation.155 | custom fusion | bytes 516
  105.1 1.6 gather_fusion.3
  106.7 1.1 reshape.334
  107.9 1.9 broadcast_select_fusion
  109.7 12.1 %all-to-all-start = ((bf16[64,2,1536]{2,1,0:T(2,128)(2,1)}), bf16[64,2,1536]{2,1,0:T(2,128)(2,1)S(1)}, u32[]{:S(2)}, u32[]{:S(2)}) async-start(bf16[64,2,1536]{2,1,0:T(2,128)(2,1)} %broadcast_select_fusion), calls=%async_computation | async-start | bytes 786432 | tf_op jit(solution)/shard_map/all_to_all | solution.py:47
  122.9 1.3 compare_select_fusion.6
  124.7 3.2 scatter_custom_fusion
  128.0 1.2 broadcast_compare_fusion.3
  130.5 2.1 gather_fusion.1
  132.6 2.2 gather_fusion.4
  138.5 1.8 and_select_fusion
  140.3 1.6 gather_fusion.5
  142.2 2.3 gather_fusion.6
  144.5 1.2 gather.47
  145.7 1.2 fusion.3
  146.9 1.2 convolution_convert_fusion.1
  148.2 1.5 convolution_convert_fusion
  149.7 1.4 copy.125
  151.1 29.8 %all_to_all.20 = bf16[16,512,128]{2,0,1:T(8,128)(2,1)} all-to-all(bf16[16,512,128]{2,0,1:T(8,128)(2,1)S(1)} %copy.125), channel_id=1, replica_groups=mesh['elem'=64,'snap'=4] {'snap'}, dimensions={1} | all-to-all | bytes 4194304 | tf_op jit(solution)/shard_map/all_to_all | solution.py:69
  180.9 5.1 copy.126
  186.0 4.5 fusion
  191.3 1.1 fusion.28
  192.4 4.5 copy.127
  197.0 4.3 dot_general.24
  201.3 248.6 %all-reduce.3.cloned.1.call-done = f32[512,512]{0,1:T(8,128)} async-done(((f32[512,512]{0,1:T(8,128)}), f32[512,512]{0,1:T(8,128)}) %all-reduce.3.cloned.1.call-update) | async-done | bytes 1048592 | tf_op jit(solution)/shard_map/psum | solution.py:76
  449.8 2.3 broadcast_multiply_fusion
  452.1 2.5 copy.129
  454.6 1.8 fusion.11
  457.4 11.7 %cholesky.104 = f32[128,128]{1,0:T(8,128)S(1)} custom-call(f32[128,128]{1,0:T(8,128)S(1)} %cholesky.266), custom_call_target="Cholesky" | custom-call | tf_op jit(solution)/shard_map/jit(cholesky)/cholesky | solution.py:78
  469.7 9.8 %custom-call.31 = f32[1,128,128]{1,2,0:T(8,128)S(1)} custom-call(f32[1,128,128]{2,1,0:T(8,128)S(1)} %get-tuple-element.47), custom_call_target="InvertDiagBlocksLowerTriangular" | custom-call | tf_op jit(solution)/shard_map/jit(cholesky)/cholesky | solution.py:78
  479.6 1.3 fusion.37
  480.9 2.1 convolution_subtract_fusion.3
  484.0 11.7 %cholesky.217 = f32[128,128]{1,0:T(8,128)S(1)} custom-call(f32[128,128]{1,0:T(8,128)S(1)} %cholesky.270), custom_call_target="Cholesky" | custom-call | tf_op jit(solution)/shard_map/jit(cholesky)/cholesky | solution.py:78
  495.7 2.0 cholesky.224
  499.0 10.2 %custom-call.32 = f32[1,128,128]{1,2,0:T(8,128)S(1)} custom-call(f32[1,128,128]{2,1,0:T(8,128)S(1)} %get-tuple-element.44), custom_call_target="InvertDiagBlocksLowerTriangular" | custom-call | tf_op jit(solution)/shard_map/jit(cholesky)/cholesky | solution.py:78
  509.2 1.8 convolution_dynamic-update-slice_fusion
  511.0 1.4 convolution_subtract_fusion.4
  512.5 11.7 %cholesky.238 = f32[128,128]{1,0:T(8,128)S(1)} custom-call(f32[128,128]{1,0:T(8,128)S(1)} %cholesky.275), custom_call_target="Cholesky" | custom-call | tf_op jit(solution)/shard_map/jit(cholesky)/cholesky | solution.py:78
  525.5 9.8 %custom-call.33 = f32[1,128,128]{1,2,0:T(8,128)S(1)} custom-call(f32[1,128,128]{2,1,0:T(8,128)S(1)} %get-tuple-element.41), custom_call_target="InvertDiagBlocksLowerTriangular" | custom-call | tf_op jit(solution)/shard_map/jit(cholesky)/cholesky | solution.py:78
  536.1 1.4 convolution_subtract_fusion.5
  537.6 11.9 %cholesky.255 = f32[128,128]{1,0:T(8,128)S(1)} custom-call(f32[128,128]{1,0:T(8,128)S(1)} %convolution_subtract_fusion.5), custom_call_target="Cholesky" | custom-call | tf_op jit(solution)/shard_map/jit(cholesky)/cholesky | solution.py:78
  553.9 2.5 fusion.12
  557.2 13.5 %while.1 = (s32[]{:T(128)}, f32[512,512]{1,0:T(8,128)}, s32[4,2]{0,1:T(2,128)S(1)}, f32[4,128,128]{2,1,0:T(8,128)}, s32[]{:T(128)}) while((s32[]{:T(128)}, f32[512,512]{1,0:T(8,128)}, s32[4,2]{0,1:T(2,128)S(1)}, f32[4,128,128]{2,1,0:T(8,128)}, s32[]{:T(128)}) %tuple.39), condition=%wide.while_cond, body=%wide.while_body.sunk | while | flops 2 | bytes 132205 | solution.py:80
  557.8 2.8 bitcast_dynamic-update-slice_fusion.2
  561.2 2.8 bitcast_dynamic-update-slice_fusion.2
  564.6 2.8 bitcast_dynamic-update-slice_fusion.2
  568.0 2.7 bitcast_dynamic-update-slice_fusion.2
  570.7 40.1 %custom-call.34 = f32[4,128,128]{1,2,0:T(8,128)S(1)} custom-call(f32[4,128,128]{2,1,0:T(8,128)} %get-tuple-element.9), custom_call_target="InvertDiagBlocksLowerTriangular" | custom-call | tf_op jit(solution)/shard_map/jit(_solve_triangular)/triangular_solve | solution.py:80
  611.9 1.4 convolution_subtract_fusion.1
  613.7 1.6 convolution_subtract_fusion
  615.8 1.7 convolution_subtract_fusion.2
  617.9 5.1 fusion.4
  (97 shorter events, 30.2 us)
Async XLA Ops:
  7.2 97.9 %copy-start = (bf16[1024,1536]{1,0:T(8,128)(2,1)S(1)}, bf16[1024,1536]{1,0:T(8,128)(2,1)}, u32[]{:S(2)}) copy-start(bf16[1024,1536]{1,0:T(8,128)(2,1)} %param.7) | copy-start | bytes 9437188
  8.0 7.9 %copy-start.1 = (s32[65536]{0:T(1024)S(1)}, s32[65536]{0:T(1024)}, u32[]{:S(2)}) copy-start(s32[65536]{0:T(1024)} %param.12) | copy-start | bytes 786436
  39.0 8.6 %copy-start.8 = (s32[512]{0:T(512)S(1)}, s32[512]{0:T(512)}, u32[]{:S(2)}) copy-start(s32[512]{0:T(512)} %param.13) | copy-start | bytes 6148
  40.0 1.9 copy-start.5
  41.9 40.0 %copy-start.6 = (pred[512,8]{1,0:T(8,128)(4,1)}, pred[512,8]{1,0:T(8,128)(4,1)S(1)}, u32[]{:S(2)}) copy-start(pred[512,8]{1,0:T(8,128)(4,1)S(1)} %get-tuple-element.33) | copy-start | bytes 12292
  43.1 1.3 copy-start.4
  47.9 38.2 %copy-start.10 = (s32[2]{0:T(128)S(1)}, s32[2]{0:T(128)}, u32[]{:S(2)}) copy-start(s32[2]{0:T(128)} %constant.235) | copy-start | bytes 28
  48.0 38.2 %copy-start.9 = (s32[2]{0:T(128)S(1)}, s32[2]{0:T(128)}, u32[]{:S(2)}) copy-start(s32[2]{0:T(128)} %constant.232) | copy-start | bytes 28
  109.7 32.5 %all-to-all-start = ((bf16[64,2,1536]{2,1,0:T(2,128)(2,1)}), bf16[64,2,1536]{2,1,0:T(2,128)(2,1)S(1)}, u32[]{:S(2)}, u32[]{:S(2)}) async-start(bf16[64,2,1536]{2,1,0:T(2,128)(2,1)} %broadcast_select_fusion), calls=%async_computation | async-start | bytes 786432 | tf_op jit(solution)/shard_map/all_to_all | solution.py:47
  121.8 328.0 %all-reduce.3.cloned.1.call-start = ((), (), s32[]{:S(2)}) async-start(), calls=%async_computation.2 | async-start | bytes 2097152 | tf_op jit(solution)/shard_map/psum | solution.py:76
  456.4 1.0 copy-start.3
  469.1 0.6 copy-start.7
  613.3 4.6 copy-start.2
Sparse Core Ops, SparseCore 0:
  190.6 259.1 all-reduce.2
where the time goes:
time: 638 us; the launch traced here: 630 us
  waiting for transfers between devices  249 us (39%)
  other arithmetic  149 us (23%)
  local copies, waits for them, and re-layouts  143 us (22%)
  matrix products  29.9 us (5%)
  blocking collectives  29.8 us (5%)
  between operations  17.2 us (3%)
  starting transfers between devices  12.1 us (2%)
    psum x1, waiting for transfers between devices, shards(): gram_matrix = lax.psum(partial_gram, ('elem', 'snap'))  249 us
    another operation x14, other arithmetic, shards(): lower_factor = jnp.linalg.cholesky(gram_matrix)  80.7 us
    another operation x3, other arithmetic, shards(): jax.scipy.linalg.solve_triangular(lower_factor, identity_matrix, lower=True)  42.6 us
    gather x4, local copies, waits for them, and re-layouts, shards(): peer_ranks = jnp.take_along_axis(ranks_by_owner, owners, axis=1)  35.9 us
    all_to_all x1, blocking collectives, shards(): lax.all_to_all(projected, 'snap', split_axis=1, concat_axis=2, tiled=True)  29.8 us
    gather x3, local copies, waits for them, and re-layouts, shards(): stored_rows = jnp.where(live_nodes, node_slot[jnp.maximum(node_ids, 0)], 0)  24.1 us
    unnamed x28, local copies, waits for them, and re-layouts  21.4 us
    another operation x12, local copies, waits for them, and re-layouts  13.5 us
  transfers between devices with their start and end apart: 2, of which 1 were waited for; matrix products, arithmetic and copies ran while one was open for 5% of the time, Pallas kernels for 0%

commit v1 on v0

--- a/solution.py
+++ b/solution.py
@@ -73,7 +73,7 @@
     partial_gram = lax.dot_general(
         band_rows, band_rows, (((0,), (0,)), ((), ())), preferred_element_type=jnp.float32
     )
-    gram_matrix = lax.psum(partial_gram, ("elem", "snap"))
+    gram_matrix = lax.psum(lax.psum(partial_gram, "snap"), "elem")
     gram_matrix = gram_matrix / total_rows
     lower_factor = jnp.linalg.cholesky(gram_matrix)
     identity_matrix = jnp.eye(columns, dtype=jnp.float32)

time: 638 us -> 623 us (0.976)
  waiting for transfers between devices: 249 us -> 233 us
    psum x1 -> x2, waiting for transfers between devices: 249 us -> 233 us  [shards(): gram_matrix = lax.psum(lax.psum(partial_gram, 'snap'), 'elem')]
  transfers between devices with their start and end apart: 2 -> 3, of which waited for: 1 -> 2; matrix products, arithmetic and copies ran while one was open for 5% -> 5% of each run, Pallas kernels for 0% -> 0%
where the time goes in v1:
time: 623 us; the launch traced here: 614 us
  waiting for transfers between devices  233 us (37%)
  other arithmetic  149 us (24%)
  local copies, waits for them, and re-layouts  143 us (23%)
  matrix products  29.9 us (5%)
  blocking collectives  29.8 us (5%)
  between operations  17.2 us (3%)
  starting transfers between devices  12.2 us (2%)
    psum x2, waiting for transfers between devices, shards(): gram_matrix = lax.psum(lax.psum(partial_gram, 'snap'), 'elem')  233 us
    another operation x14, other arithmetic, shards(): lower_factor = jnp.linalg.cholesky(gram_matrix)  80.7 us
    another operation x3, other arithmetic, shards(): jax.scipy.linalg.solve_triangular(lower_factor, identity_matrix, lower=True)  42.6 us
    gather x4, local copies, waits for them, and re-layouts, shards(): peer_ranks = jnp.take_along_axis(ranks_by_owner, owners, axis=1)  35.9 us
    all_to_all x1, blocking collectives, shards(): lax.all_to_all(projected, 'snap', split_axis=1, concat_axis=2, tiled=True)  29.8 us
    gather x3, local copies, waits for them, and re-layouts, shards(): stored_rows = jnp.where(live_nodes, node_slot[jnp.maximum(node_ids, 0)], 0)  24.1 us
    unnamed x28, local copies, waits for them, and re-layouts  21.4 us
    another operation x12, local copies, waits for them, and re-layouts  13.5 us
  transfers between devices with their start and end apart: 3, of which 2 were waited for; matrix products, arithmetic and copies ran while one was open for 5% of the time, Pallas kernels for 0%

profile of v1, /device:TPU:2, one launch (start us, length us, event | category | flops | bytes accessed | tf_op | source)
XLA Modules:
  0.0 614.4 jit_solution(17505741598922533651)
XLA Ops:
  8.0 2.3 copy.109
  10.3 2.9 gather_fusion
  13.2 1.7 broadcast_maximum_fusion
  14.8 1.1 reshape.327
  15.9 23.0 %gather_fusion.2 = s32[4096]{0:T(1024)S(1)} fusion(s32[65536]{0:T(1024)S(1)} %copy-done.1, s32[4096]{0:T(1024)S(1)} %broadcast_clamp_fusion), kind=kCustom, calls=%fused_computation.2 | custom fusion | bytes 49152 | tf_op jit(solution)/shard_map/gather | solution.py:22
  40.0 1.9 add_select_fusion
  41.9 1.1 add_select_fusion.1
  43.2 1.1 reshape.379
  44.4 1.9 shift-left_or_fusion
  48.0 33.0 %gather_fusion.7 = s32[4096]{0:T(1024)S(1)} fusion(s32[512,64]{0,1:T(8,128)S(1)} %convolution_convert_fusion.2, s32[4096]{0:T(1024)S(1)} %reshape.363), kind=kCustom, calls=%fused_computation.7 | custom fusion | bytes 65536 | tf_op jit(solution)/shard_map/jit(take_along_axis)/gather | solution.py:37
  81.9 2.1 compare_select_fusion.3
  88.4 15.5 %scatter_custom_fusion.1 = s32[128]{0:T(128)S(1)} fusion(s32[4096]{0:T(1024)S(1)} %reshape.377, s32[4096]{0:T(1024)S(1)} %reshape.379, s32[]{:T(128)} %constant.211.clone.1), kind=kCustom, calls=%fused_computation.155 | custom fusion | bytes 516
  105.1 1.6 gather_fusion.3
  106.7 1.1 reshape.334
  107.9 1.9 broadcast_select_fusion
  109.7 12.1 %all-to-all-start = ((bf16[64,2,1536]{2,1,0:T(2,128)(2,1)}), bf16[64,2,1536]{2,1,0:T(2,128)(2,1)S(1)}, u32[]{:S(2)}, u32[]{:S(2)}) async-start(bf16[64,2,1536]{2,1,0:T(2,128)(2,1)} %broadcast_select_fusion), calls=%async_computation | async-start | bytes 786432 | tf_op jit(solution)/shard_map/all_to_all | solution.py:47
  122.9 1.3 compare_select_fusion.6
  124.7 3.2 scatter_custom_fusion
  128.0 1.2 broadcast_compare_fusion.3
  130.5 2.1 gather_fusion.1
  132.6 2.2 gather_fusion.4
  138.5 1.8 and_select_fusion
  140.3 1.6 gather_fusion.5
  142.2 2.3 gather_fusion.6
  144.5 1.2 gather.47
  145.7 1.2 fusion.3
  146.9 1.2 convolution_convert_fusion.1
  148.2 1.5 convolution_convert_fusion
  149.7 1.4 copy.125
  151.1 29.8 %all_to_all.20 = bf16[16,512,128]{2,0,1:T(8,128)(2,1)} all-to-all(bf16[16,512,128]{2,0,1:T(8,128)(2,1)S(1)} %copy.125), channel_id=1, replica_groups=mesh['elem'=64,'snap'=4] {'snap'}, dimensions={1} | all-to-all | bytes 4194304 | tf_op jit(solution)/shard_map/all_to_all | solution.py:69
  180.9 5.1 copy.126
  186.0 4.5 fusion
  190.6 51.0 %all-reduce.4.cloned.1.call-done = f32[512,512]{0,1:T(8,128)} async-done(((f32[512,512]{0,1:T(8,128)}), f32[512,512]{0,1:T(8,128)}) %all-reduce.4.cloned.1.call-update) | async-done | bytes 1048592 | tf_op jit(solution)/shard_map/psum | solution.py:76
  242.4 1.1 fusion.28
  243.5 4.5 copy.127
  248.0 4.3 dot_general.24
  252.3 181.9 %all-reduce.6.cloned.1.call-done = f32[512,512]{0,1:T(8,128)} async-done(((f32[512,512]{0,1:T(8,128)}), f32[512,512]{0,1:T(8,128)}) %all-reduce.6.cloned.1.call-update) | async-done | bytes 1048592 | tf_op jit(solution)/shard_map/psum | solution.py:76
  434.2 2.3 broadcast_multiply_fusion
  436.5 2.5 copy.129
  439.0 1.8 fusion.11
  441.8 11.7 %cholesky.104 = f32[128,128]{1,0:T(8,128)S(1)} custom-call(f32[128,128]{1,0:T(8,128)S(1)} %cholesky.266), custom_call_target="Cholesky" | custom-call | tf_op jit(solution)/shard_map/jit(cholesky)/cholesky | solution.py:78
  454.1 9.8 %custom-call.31 = f32[1,128,128]{1,2,0:T(8,128)S(1)} custom-call(f32[1,128,128]{2,1,0:T(8,128)S(1)} %get-tuple-element.47), custom_call_target="InvertDiagBlocksLowerTriangular" | custom-call | tf_op jit(solution)/shard_map/jit(cholesky)/cholesky | solution.py:78
  464.0 1.3 fusion.37
  465.3 2.1 convolution_subtract_fusion.3
  468.4 11.7 %cholesky.217 = f32[128,128]{1,0:T(8,128)S(1)} custom-call(f32[128,128]{1,0:T(8,128)S(1)} %cholesky.270), custom_call_target="Cholesky" | custom-call | tf_op jit(solution)/shard_map/jit(cholesky)/cholesky | solution.py:78
  480.1 2.0 cholesky.224
  483.4 10.2 %custom-call.32 = f32[1,128,128]{1,2,0:T(8,128)S(1)} custom-call(f32[1,128,128]{2,1,0:T(8,128)S(1)} %get-tuple-element.44), custom_call_target="InvertDiagBlocksLowerTriangular" | custom-call | tf_op jit(solution)/shard_map/jit(cholesky)/cholesky | solution.py:78
  493.6 1.8 convolution_dynamic-update-slice_fusion
  495.4 1.4 convolution_subtract_fusion.4
  496.9 11.7 %cholesky.238 = f32[128,128]{1,0:T(8,128)S(1)} custom-call(f32[128,128]{1,0:T(8,128)S(1)} %cholesky.275), custom_call_target="Cholesky" | custom-call | tf_op jit(solution)/shard_map/jit(cholesky)/cholesky | solution.py:78
  509.9 9.8 %custom-call.33 = f32[1,128,128]{1,2,0:T(8,128)S(1)} custom-call(f32[1,128,128]{2,1,0:T(8,128)S(1)} %get-tuple-element.41), custom_call_target="InvertDiagBlocksLowerTriangular" | custom-call | tf_op jit(solution)/shard_map/jit(cholesky)/cholesky | solution.py:78
  520.5 1.4 convolution_subtract_fusion.5
  522.0 11.9 %cholesky.255 = f32[128,128]{1,0:T(8,128)S(1)} custom-call(f32[128,128]{1,0:T(8,128)S(1)} %convolution_subtract_fusion.5), custom_call_target="Cholesky" | custom-call | tf_op jit(solution)/shard_map/jit(cholesky)/cholesky | solution.py:78
  538.3 2.5 fusion.12
  541.6 13.5 %while.1 = (s32[]{:T(128)}, f32[512,512]{1,0:T(8,128)}, s32[4,2]{0,1:T(2,128)S(1)}, f32[4,128,128]{2,1,0:T(8,128)}, s32[]{:T(128)}) while((s32[]{:T(128)}, f32[512,512]{1,0:T(8,128)}, s32[4,2]{0,1:T(2,128)S(1)}, f32[4,128,128]{2,1,0:T(8,128)}, s32[]{:T(128)}) %tuple.39), condition=%wide.while_cond, body=%wide.while_body.sunk | while | flops 2 | bytes 132205 | solution.py:80
  542.2 2.8 bitcast_dynamic-update-slice_fusion.2
  545.6 2.8 bitcast_dynamic-update-slice_fusion.2
  549.0 2.8 bitcast_dynamic-update-slice_fusion.2
  552.4 2.7 bitcast_dynamic-update-slice_fusion.2
  555.1 40.1 %custom-call.34 = f32[4,128,128]{1,2,0:T(8,128)S(1)} custom-call(f32[4,128,128]{2,1,0:T(8,128)} %get-tuple-element.9), custom_call_target="InvertDiagBlocksLowerTriangular" | custom-call | tf_op jit(solution)/shard_map/jit(_solve_triangular)/triangular_solve | solution.py:80
  596.3 1.4 convolution_subtract_fusion.1
  598.1 1.6 convolution_subtract_fusion
  600.2 1.7 convolution_subtract_fusion.2
  602.3 5.1 fusion.4
  (100 shorter events, 31.4 us)
Async XLA Ops:
  7.2 97.9 %copy-start = (bf16[1024,1536]{1,0:T(8,128)(2,1)S(1)}, bf16[1024,1536]{1,0:T(8,128)(2,1)}, u32[]{:S(2)}) copy-start(bf16[1024,1536]{1,0:T(8,128)(2,1)} %param.7) | copy-start | bytes 9437188
  8.0 7.9 %copy-start.1 = (s32[65536]{0:T(1024)S(1)}, s32[65536]{0:T(1024)}, u32[]{:S(2)}) copy-start(s32[65536]{0:T(1024)} %param.12) | copy-start | bytes 786436
  39.0 8.6 %copy-start.8 = (s32[512]{0:T(512)S(1)}, s32[512]{0:T(512)}, u32[]{:S(2)}) copy-start(s32[512]{0:T(512)} %param.13) | copy-start | bytes 6148
  40.0 1.9 copy-start.5
  41.9 40.0 %copy-start.6 = (pred[512,8]{1,0:T(8,128)(4,1)}, pred[512,8]{1,0:T(8,128)(4,1)S(1)}, u32[]{:S(2)}) copy-start(pred[512,8]{1,0:T(8,128)(4,1)S(1)} %get-tuple-element.33) | copy-start | bytes 12292
  43.1 1.3 copy-start.4
  47.9 38.2 %copy-start.10 = (s32[2]{0:T(128)S(1)}, s32[2]{0:T(128)}, u32[]{:S(2)}) copy-start(s32[2]{0:T(128)} %constant.235) | copy-start | bytes 28
  48.0 38.2 %copy-start.9 = (s32[2]{0:T(128)S(1)}, s32[2]{0:T(128)}, u32[]{:S(2)}) copy-start(s32[2]{0:T(128)} %constant.232) | copy-start | bytes 28
  109.7 32.5 %all-to-all-start = ((bf16[64,2,1536]{2,1,0:T(2,128)(2,1)}), bf16[64,2,1536]{2,1,0:T(2,128)(2,1)S(1)}, u32[]{:S(2)}, u32[]{:S(2)}) async-start(bf16[64,2,1536]{2,1,0:T(2,128)(2,1)} %broadcast_select_fusion), calls=%async_computation | async-start | bytes 786432 | tf_op jit(solution)/shard_map/all_to_all | solution.py:47
  121.8 119.7 %all-reduce.4.cloned.1.call-start = ((), (), s32[]{:S(2)}) async-start(), calls=%async_computation.2 | async-start | bytes 2097152 | tf_op jit(solution)/shard_map/psum | solution.py:76
  190.5 243.7 %all-reduce.6.cloned.1.call-start = ((), (), s32[]{:S(2)}) async-start(), calls=%async_computation.3 | async-start | bytes 2097152 | tf_op jit(solution)/shard_map/psum | solution.py:76
  440.8 1.0 copy-start.3
  453.5 0.6 copy-start.7
  597.7 4.6 copy-start.2
Sparse Core Ops, SparseCore 0:
  190.6 50.8 all-reduce.3
  245.0 189.1 all-reduce.5
